TPU v7x, 256 devices: a whole 4x4x8 slice. The times are simulated.
256 devices in a mesh: pairs: 32 (over z, y_hi, core), aux: 8 (over x, y_lo).
Axes of the slice: x: 4, y: 4 (y_hi: 2, y_lo: 2; y = y_hi * 2 + y_lo), z: 8, core: 2. Of those that a mesh axis runs over, the one named last changes fastest.
Arguments:
- amplitudes: float32 [64, 256, 256], P('pairs'), may hold values from -6 to 6
- factors: float32 [384, 256, 256], P('aux', 'pairs'), may hold values from -0.078125 to 0.078125
- occ_factors: float32 [384, 8, 8], P('aux'), may hold values from -0.5 to 0.5
Outputs:
- resid: float32 [64, 256, 256], P(None, 'pairs', 'aux')
All inputs are finite; a program needn't handle non-finite values.
Results may differ from a plain program's by a relative error of at most 0.0001.
Values sent between devices are 32-bit elements; how exact they have to be, the bound alone decides.
A program may use at most 64 MiB of HBM per device.

v0:
```python
import jax
import jax.numpy as jnp
from jax import lax
from jax.sharding import PartitionSpec as P

highest = lax.Precision.HIGHEST


def both_sides(running, amps, row_block):
    mixed_terms = jnp.einsum("icd,pbd->picb", amps, row_block, precision=highest)
    return running + jnp.einsum("pac,picb->iab", row_block, mixed_terms, precision=highest)


def shards(amplitudes, factors, occ_factors):
    local_pairs = amplitudes.shape[0]
    virt_width = amplitudes.shape[1]
    aux_local = factors.shape[0]
    occupied = occ_factors.shape[1]
    total_pairs = occupied * occupied
    aux_rank = lax.axis_index("aux")
    column_count = virt_width // lax.axis_size("aux")
    col_start = aux_rank * column_count
    amp_cols = lax.dynamic_slice_in_dim(amplitudes, col_start, column_count, 2)
    amp_flip = jnp.swapaxes(lax.dynamic_slice_in_dim(amplitudes, col_start, column_count, 1), 1, 2)

    def whole_step(running, block_index):
        row_block = lax.dynamic_slice_in_dim(factors, block_index * 2, 2, 0)
        whole_rows = lax.all_gather(row_block, "pairs", axis=1, tiled=True)
        return (both_sides(running, amplitudes, whole_rows), None)

    particle, unused = lax.scan(
        whole_step,
        jnp.zeros((local_pairs, virt_width, virt_width), jnp.float32),
        jnp.arange(aux_local // 2),
    )
    coupling = jnp.einsum("pik,pjl->ijkl", occ_factors, occ_factors, precision=highest).reshape(
        total_pairs, total_pairs
    )
    particle, coupling = lax.psum((particle, coupling), "aux")
    part_cols = lax.dynamic_slice_in_dim(particle, col_start, column_count, 2)
    part_flip = jnp.swapaxes(lax.dynamic_slice_in_dim(particle, col_start, column_count, 1), 1, 2)
    part_cols, part_flip, amp_cols, amp_flip = (
        lax.all_to_all(part_cols, "pairs", split_axis=1, concat_axis=0, tiled=True),
        lax.all_to_all(part_flip, "pairs", split_axis=1, concat_axis=0, tiled=True),
        lax.all_to_all(amp_cols, "pairs", split_axis=1, concat_axis=0, tiled=True),
        lax.all_to_all(amp_flip, "pairs", split_axis=1, concat_axis=0, tiled=True),
    )
    straight = part_cols + jnp.einsum("pk,kab->pab", coupling, amp_cols, precision=highest)
    turned = part_flip + jnp.einsum("pk,kab->pab", coupling, amp_flip, precision=highest)
    rows_here = turned.shape[1]
    turned = (
        turned.reshape(occupied, occupied, rows_here, column_count)
        .transpose(1, 0, 2, 3)
        .reshape(total_pairs, rows_here, column_count)
    )
    return straight + turned


def solution(mesh):
    placed = (P("pairs", None, None), P("aux", "pairs", None), P("aux", None, None))
    return jax.shard_map(
        shards, mesh=mesh, in_specs=placed, out_specs=P(None, "pairs", "aux"), check_vma=False
    )
```

profile of v0, /device:TPU:1, one launch (start us, length us, event | category | flops | bytes accessed | tf_op | source)
XLA Modules:
  0.0 1193.5 jit_solution(1170505517774073015)
XLA Ops:
  6.5 1064.0 %while.11 = (s32[]{:T(128)}, f32[2,256,256]{1,2,0:T(8,128)S(1)}, s32[24]{0:T(128)S(1)}, f32[48,8,256]{2,1,0:T(8,128)}, f32[2,256,256]{2,1,0:T(8,128)}, /*index=5*/s32[]{:T(128)}, s32[1]{0:T(128)}, s32[]{:T(128)}, s32[]{:T(128)}) while((s32[]{:T(128)}, f32[2,256,256]{1,2,0:T(8,128)S(1)}, s32[24]{0:T(128)S(1)}, ...), condition=%wide.region_1.2_spmd.clone, body=%wide.region_0.1_spmd.clone.sunk | while | flops 1610874880 | bytes 7389385 | solution.py:31
  8.6 47.7 %all_gather.5 = f32[2,256,256]{2,1,0:T(8,128)S(1)} all-gather(f32[2,8,256]{2,1,0:T(8,128)S(1)} %constant_dynamic-slice_fusion.5), channel_id=1, replica_groups=mesh['pairs'=32,'aux'=8] {'pairs'}, dimensions={1}, use_global_device_ids=true | all-gather | bytes 540672 | tf_op jit(solution)/shard_map/while/body/eval_jaxpr/all_gather | solution.py:28
  60.8 38.1 %all_gather.5 = f32[2,256,256]{2,1,0:T(8,128)S(1)} all-gather(f32[2,8,256]{2,1,0:T(8,128)S(1)} %constant_dynamic-slice_fusion.5), channel_id=1, replica_groups=mesh['pairs'=32,'aux'=8] {'pairs'}, dimensions={1}, use_global_device_ids=true | all-gather | bytes 540672 | tf_op jit(solution)/shard_map/while/body/eval_jaxpr/all_gather | solution.py:28
  103.3 41.1 %all_gather.5 = f32[2,256,256]{2,1,0:T(8,128)S(1)} all-gather(f32[2,8,256]{2,1,0:T(8,128)S(1)} %constant_dynamic-slice_fusion.5), channel_id=1, replica_groups=mesh['pairs'=32,'aux'=8] {'pairs'}, dimensions={1}, use_global_device_ids=true | all-gather | bytes 540672 | tf_op jit(solution)/shard_map/while/body/eval_jaxpr/all_gather | solution.py:28
  148.9 38.1 %all_gather.5 = f32[2,256,256]{2,1,0:T(8,128)S(1)} all-gather(f32[2,8,256]{2,1,0:T(8,128)S(1)} %constant_dynamic-slice_fusion.5), channel_id=1, replica_groups=mesh['pairs'=32,'aux'=8] {'pairs'}, dimensions={1}, use_global_device_ids=true | all-gather | bytes 540672 | tf_op jit(solution)/shard_map/while/body/eval_jaxpr/all_gather | solution.py:28
  191.5 41.1 %all_gather.5 = f32[2,256,256]{2,1,0:T(8,128)S(1)} all-gather(f32[2,8,256]{2,1,0:T(8,128)S(1)} %constant_dynamic-slice_fusion.5), channel_id=1, replica_groups=mesh['pairs'=32,'aux'=8] {'pairs'}, dimensions={1}, use_global_device_ids=true | all-gather | bytes 540672 | tf_op jit(solution)/shard_map/while/body/eval_jaxpr/all_gather | solution.py:28
  237.0 38.1 %all_gather.5 = f32[2,256,256]{2,1,0:T(8,128)S(1)} all-gather(f32[2,8,256]{2,1,0:T(8,128)S(1)} %constant_dynamic-slice_fusion.5), channel_id=1, replica_groups=mesh['pairs'=32,'aux'=8] {'pairs'}, dimensions={1}, use_global_device_ids=true | all-gather | bytes 540672 | tf_op jit(solution)/shard_map/while/body/eval_jaxpr/all_gather | solution.py:28
  279.6 41.1 %all_gather.5 = f32[2,256,256]{2,1,0:T(8,128)S(1)} all-gather(f32[2,8,256]{2,1,0:T(8,128)S(1)} %constant_dynamic-slice_fusion.5), channel_id=1, replica_groups=mesh['pairs'=32,'aux'=8] {'pairs'}, dimensions={1}, use_global_device_ids=true | all-gather | bytes 540672 | tf_op jit(solution)/shard_map/while/body/eval_jaxpr/all_gather | solution.py:28
  325.1 38.1 %all_gather.5 = f32[2,256,256]{2,1,0:T(8,128)S(1)} all-gather(f32[2,8,256]{2,1,0:T(8,128)S(1)} %constant_dynamic-slice_fusion.5), channel_id=1, replica_groups=mesh['pairs'=32,'aux'=8] {'pairs'}, dimensions={1}, use_global_device_ids=true | all-gather | bytes 540672 | tf_op jit(solution)/shard_map/while/body/eval_jaxpr/all_gather | solution.py:28
  367.7 41.1 %all_gather.5 = f32[2,256,256]{2,1,0:T(8,128)S(1)} all-gather(f32[2,8,256]{2,1,0:T(8,128)S(1)} %constant_dynamic-slice_fusion.5), channel_id=1, replica_groups=mesh['pairs'=32,'aux'=8] {'pairs'}, dimensions={1}, use_global_device_ids=true | all-gather | bytes 540672 | tf_op jit(solution)/shard_map/while/body/eval_jaxpr/all_gather | solution.py:28
  413.3 38.1 %all_gather.5 = f32[2,256,256]{2,1,0:T(8,128)S(1)} all-gather(f32[2,8,256]{2,1,0:T(8,128)S(1)} %constant_dynamic-slice_fusion.5), channel_id=1, replica_groups=mesh['pairs'=32,'aux'=8] {'pairs'}, dimensions={1}, use_global_device_ids=true | all-gather | bytes 540672 | tf_op jit(solution)/shard_map/while/body/eval_jaxpr/all_gather | solution.py:28
  455.8 41.1 %all_gather.5 = f32[2,256,256]{2,1,0:T(8,128)S(1)} all-gather(f32[2,8,256]{2,1,0:T(8,128)S(1)} %constant_dynamic-slice_fusion.5), channel_id=1, replica_groups=mesh['pairs'=32,'aux'=8] {'pairs'}, dimensions={1}, use_global_device_ids=true | all-gather | bytes 540672 | tf_op jit(solution)/shard_map/while/body/eval_jaxpr/all_gather | solution.py:28
  501.4 38.1 %all_gather.5 = f32[2,256,256]{2,1,0:T(8,128)S(1)} all-gather(f32[2,8,256]{2,1,0:T(8,128)S(1)} %constant_dynamic-slice_fusion.5), channel_id=1, replica_groups=mesh['pairs'=32,'aux'=8] {'pairs'}, dimensions={1}, use_global_device_ids=true | all-gather | bytes 540672 | tf_op jit(solution)/shard_map/while/body/eval_jaxpr/all_gather | solution.py:28
  543.9 41.1 %all_gather.5 = f32[2,256,256]{2,1,0:T(8,128)S(1)} all-gather(f32[2,8,256]{2,1,0:T(8,128)S(1)} %constant_dynamic-slice_fusion.5), channel_id=1, replica_groups=mesh['pairs'=32,'aux'=8] {'pairs'}, dimensions={1}, use_global_device_ids=true | all-gather | bytes 540672 | tf_op jit(solution)/shard_map/while/body/eval_jaxpr/all_gather | solution.py:28
  589.5 38.1 %all_gather.5 = f32[2,256,256]{2,1,0:T(8,128)S(1)} all-gather(f32[2,8,256]{2,1,0:T(8,128)S(1)} %constant_dynamic-slice_fusion.5), channel_id=1, replica_groups=mesh['pairs'=32,'aux'=8] {'pairs'}, dimensions={1}, use_global_device_ids=true | all-gather | bytes 540672 | tf_op jit(solution)/shard_map/while/body/eval_jaxpr/all_gather | solution.py:28
  632.1 41.1 %all_gather.5 = f32[2,256,256]{2,1,0:T(8,128)S(1)} all-gather(f32[2,8,256]{2,1,0:T(8,128)S(1)} %constant_dynamic-slice_fusion.5), channel_id=1, replica_groups=mesh['pairs'=32,'aux'=8] {'pairs'}, dimensions={1}, use_global_device_ids=true | all-gather | bytes 540672 | tf_op jit(solution)/shard_map/while/body/eval_jaxpr/all_gather | solution.py:28
  677.6 38.1 %all_gather.5 = f32[2,256,256]{2,1,0:T(8,128)S(1)} all-gather(f32[2,8,256]{2,1,0:T(8,128)S(1)} %constant_dynamic-slice_fusion.5), channel_id=1, replica_groups=mesh['pairs'=32,'aux'=8] {'pairs'}, dimensions={1}, use_global_device_ids=true | all-gather | bytes 540672 | tf_op jit(solution)/shard_map/while/body/eval_jaxpr/all_gather | solution.py:28
  720.2 41.1 %all_gather.5 = f32[2,256,256]{2,1,0:T(8,128)S(1)} all-gather(f32[2,8,256]{2,1,0:T(8,128)S(1)} %constant_dynamic-slice_fusion.5), channel_id=1, replica_groups=mesh['pairs'=32,'aux'=8] {'pairs'}, dimensions={1}, use_global_device_ids=true | all-gather | bytes 540672 | tf_op jit(solution)/shard_map/while/body/eval_jaxpr/all_gather | solution.py:28
  765.7 38.1 %all_gather.5 = f32[2,256,256]{2,1,0:T(8,128)S(1)} all-gather(f32[2,8,256]{2,1,0:T(8,128)S(1)} %constant_dynamic-slice_fusion.5), channel_id=1, replica_groups=mesh['pairs'=32,'aux'=8] {'pairs'}, dimensions={1}, use_global_device_ids=true | all-gather | bytes 540672 | tf_op jit(solution)/shard_map/while/body/eval_jaxpr/all_gather | solution.py:28
  808.3 41.1 %all_gather.5 = f32[2,256,256]{2,1,0:T(8,128)S(1)} all-gather(f32[2,8,256]{2,1,0:T(8,128)S(1)} %constant_dynamic-slice_fusion.5), channel_id=1, replica_groups=mesh['pairs'=32,'aux'=8] {'pairs'}, dimensions={1}, use_global_device_ids=true | all-gather | bytes 540672 | tf_op jit(solution)/shard_map/while/body/eval_jaxpr/all_gather | solution.py:28
  853.8 38.1 %all_gather.5 = f32[2,256,256]{2,1,0:T(8,128)S(1)} all-gather(f32[2,8,256]{2,1,0:T(8,128)S(1)} %constant_dynamic-slice_fusion.5), channel_id=1, replica_groups=mesh['pairs'=32,'aux'=8] {'pairs'}, dimensions={1}, use_global_device_ids=true | all-gather | bytes 540672 | tf_op jit(solution)/shard_map/while/body/eval_jaxpr/all_gather | solution.py:28
  896.4 41.1 %all_gather.5 = f32[2,256,256]{2,1,0:T(8,128)S(1)} all-gather(f32[2,8,256]{2,1,0:T(8,128)S(1)} %constant_dynamic-slice_fusion.5), channel_id=1, replica_groups=mesh['pairs'=32,'aux'=8] {'pairs'}, dimensions={1}, use_global_device_ids=true | all-gather | bytes 540672 | tf_op jit(solution)/shard_map/while/body/eval_jaxpr/all_gather | solution.py:28
  942.0 38.1 %all_gather.5 = f32[2,256,256]{2,1,0:T(8,128)S(1)} all-gather(f32[2,8,256]{2,1,0:T(8,128)S(1)} %constant_dynamic-slice_fusion.5), channel_id=1, replica_groups=mesh['pairs'=32,'aux'=8] {'pairs'}, dimensions={1}, use_global_device_ids=true | all-gather | bytes 540672 | tf_op jit(solution)/shard_map/while/body/eval_jaxpr/all_gather | solution.py:28
  984.5 41.1 %all_gather.5 = f32[2,256,256]{2,1,0:T(8,128)S(1)} all-gather(f32[2,8,256]{2,1,0:T(8,128)S(1)} %constant_dynamic-slice_fusion.5), channel_id=1, replica_groups=mesh['pairs'=32,'aux'=8] {'pairs'}, dimensions={1}, use_global_device_ids=true | all-gather | bytes 540672 | tf_op jit(solution)/shard_map/while/body/eval_jaxpr/all_gather | solution.py:28
  (208 shorter events, 242.6 us)
Async XLA Ops:
  6.5 1073.3 %copy-start = (f32[48,8,8]{0,2,1:T(8,128)S(1)}, f32[48,8,8]{0,2,1:T(8,128)}, u32[]{:S(2)}) copy-start(f32[48,8,8]{0,2,1:T(8,128)} %param.7) | copy-start | bytes 36868
  6.5 1137.5 %all-reduce.2.cloned.1.call-start = ((), (), s32[]{:S(2)}) async-start(), calls=%async_computation.4 | async-start | bytes 1048576 | tf_op jit(solution)/shard_map/psum | solution.py:39
  6.5 49.8 %copy-start.1 = (f32[2,256,256]{2,1,0:T(8,128)S(1)}, f32[2,256,256]{2,1,0:T(8,128)}, u32[]{:S(2)}) copy-start(f32[2,256,256]{2,1,0:T(8,128)} %get-tuple-element.114) | copy-start | bytes 1572868 | tf_op jit(solution)/shard_map/while
  101.2 43.2 %copy-start.1 = (f32[2,256,256]{2,1,0:T(8,128)S(1)}, f32[2,256,256]{2,1,0:T(8,128)}, u32[]{:S(2)}) copy-start(f32[2,256,256]{2,1,0:T(8,128)} %get-tuple-element.114) | copy-start | bytes 1572868 | tf_op jit(solution)/shard_map/while
  146.8 40.2 %copy-start.1 = (f32[2,256,256]{2,1,0:T(8,128)S(1)}, f32[2,256,256]{2,1,0:T(8,128)}, u32[]{:S(2)}) copy-start(f32[2,256,256]{2,1,0:T(8,128)} %get-tuple-element.114) | copy-start | bytes 1572868 | tf_op jit(solution)/shard_map/while
  189.4 43.2 %copy-start.1 = (f32[2,256,256]{2,1,0:T(8,128)S(1)}, f32[2,256,256]{2,1,0:T(8,128)}, u32[]{:S(2)}) copy-start(f32[2,256,256]{2,1,0:T(8,128)} %get-tuple-element.114) | copy-start | bytes 1572868 | tf_op jit(solution)/shard_map/while
  277.5 43.2 %copy-start.1 = (f32[2,256,256]{2,1,0:T(8,128)S(1)}, f32[2,256,256]{2,1,0:T(8,128)}, u32[]{:S(2)}) copy-start(f32[2,256,256]{2,1,0:T(8,128)} %get-tuple-element.114) | copy-start | bytes 1572868 | tf_op jit(solution)/shard_map/while
  323.0 40.2 %copy-start.1 = (f32[2,256,256]{2,1,0:T(8,128)S(1)}, f32[2,256,256]{2,1,0:T(8,128)}, u32[]{:S(2)}) copy-start(f32[2,256,256]{2,1,0:T(8,128)} %get-tuple-element.114) | copy-start | bytes 1572868 | tf_op jit(solution)/shard_map/while
  365.6 43.2 %copy-start.1 = (f32[2,256,256]{2,1,0:T(8,128)S(1)}, f32[2,256,256]{2,1,0:T(8,128)}, u32[]{:S(2)}) copy-start(f32[2,256,256]{2,1,0:T(8,128)} %get-tuple-element.114) | copy-start | bytes 1572868 | tf_op jit(solution)/shard_map/while
  411.1 40.2 %copy-start.1 = (f32[2,256,256]{2,1,0:T(8,128)S(1)}, f32[2,256,256]{2,1,0:T(8,128)}, u32[]{:S(2)}) copy-start(f32[2,256,256]{2,1,0:T(8,128)} %get-tuple-element.114) | copy-start | bytes 1572868 | tf_op jit(solution)/shard_map/while
  453.7 43.2 %copy-start.1 = (f32[2,256,256]{2,1,0:T(8,128)S(1)}, f32[2,256,256]{2,1,0:T(8,128)}, u32[]{:S(2)}) copy-start(f32[2,256,256]{2,1,0:T(8,128)} %get-tuple-element.114) | copy-start | bytes 1572868 | tf_op jit(solution)/shard_map/while
  499.3 40.2 %copy-start.1 = (f32[2,256,256]{2,1,0:T(8,128)S(1)}, f32[2,256,256]{2,1,0:T(8,128)}, u32[]{:S(2)}) copy-start(f32[2,256,256]{2,1,0:T(8,128)} %get-tuple-element.114) | copy-start | bytes 1572868 | tf_op jit(solution)/shard_map/while
  541.8 43.2 %copy-start.1 = (f32[2,256,256]{2,1,0:T(8,128)S(1)}, f32[2,256,256]{2,1,0:T(8,128)}, u32[]{:S(2)}) copy-start(f32[2,256,256]{2,1,0:T(8,128)} %get-tuple-element.114) | copy-start | bytes 1572868 | tf_op jit(solution)/shard_map/while
  629.9 43.2 %copy-start.1 = (f32[2,256,256]{2,1,0:T(8,128)S(1)}, f32[2,256,256]{2,1,0:T(8,128)}, u32[]{:S(2)}) copy-start(f32[2,256,256]{2,1,0:T(8,128)} %get-tuple-element.114) | copy-start | bytes 1572868 | tf_op jit(solution)/shard_map/while
  675.5 40.2 %copy-start.1 = (f32[2,256,256]{2,1,0:T(8,128)S(1)}, f32[2,256,256]{2,1,0:T(8,128)}, u32[]{:S(2)}) copy-start(f32[2,256,256]{2,1,0:T(8,128)} %get-tuple-element.114) | copy-start | bytes 1572868 | tf_op jit(solution)/shard_map/while
  718.1 43.2 %copy-start.1 = (f32[2,256,256]{2,1,0:T(8,128)S(1)}, f32[2,256,256]{2,1,0:T(8,128)}, u32[]{:S(2)}) copy-start(f32[2,256,256]{2,1,0:T(8,128)} %get-tuple-element.114) | copy-start | bytes 1572868 | tf_op jit(solution)/shard_map/while
  763.6 40.2 %copy-start.1 = (f32[2,256,256]{2,1,0:T(8,128)S(1)}, f32[2,256,256]{2,1,0:T(8,128)}, u32[]{:S(2)}) copy-start(f32[2,256,256]{2,1,0:T(8,128)} %get-tuple-element.114) | copy-start | bytes 1572868 | tf_op jit(solution)/shard_map/while
  806.2 43.2 %copy-start.1 = (f32[2,256,256]{2,1,0:T(8,128)S(1)}, f32[2,256,256]{2,1,0:T(8,128)}, u32[]{:S(2)}) copy-start(f32[2,256,256]{2,1,0:T(8,128)} %get-tuple-element.114) | copy-start | bytes 1572868 | tf_op jit(solution)/shard_map/while
  894.3 43.2 %copy-start.1 = (f32[2,256,256]{2,1,0:T(8,128)S(1)}, f32[2,256,256]{2,1,0:T(8,128)}, u32[]{:S(2)}) copy-start(f32[2,256,256]{2,1,0:T(8,128)} %get-tuple-element.114) | copy-start | bytes 1572868 | tf_op jit(solution)/shard_map/while
  982.4 43.2 %copy-start.1 = (f32[2,256,256]{2,1,0:T(8,128)S(1)}, f32[2,256,256]{2,1,0:T(8,128)}, u32[]{:S(2)}) copy-start(f32[2,256,256]{2,1,0:T(8,128)} %get-tuple-element.114) | copy-start | bytes 1572868 | tf_op jit(solution)/shard_map/while
  1073.7 15.9 %all-to-all-start.3 = ((f32[32,1,512]{2,1,0:T(1,128)}), f32[32,1,512]{2,1,0:T(1,128)S(1)}, u32[]{:S(2)}, u32[]{:S(2)}) async-start(f32[32,1,512]{2,1,0:T(1,128)} %reshape.24), calls=%async_computation.3 | async-start | bytes 131072 | tf_op jit(solution)/shard_map/all_to_all | solution.py:46
  1089.6 56.3 %all-to-all-start.1 = ((f32[32,1,512]{2,1,0:T(1,128)}), f32[32,1,512]{2,1,0:T(1,128)S(1)}, u32[]{:S(2)}, u32[]{:S(2)}) async-start(f32[32,1,512]{2,1,0:T(1,128)} %reshape.28), calls=%async_computation.1 | async-start | bytes 131072 | tf_op jit(solution)/shard_map/all_to_all | solution.py:45
  1145.9 25.0 %all-to-all-start.2 = ((f32[32,1,512]{2,1,0:T(1,128)}), f32[32,1,512]{2,1,0:T(1,128)S(1)}, u32[]{:S(2)}, u32[]{:S(2)}) async-start(f32[32,1,512]{2,1,0:T(1,128)} %reshape.22), calls=%async_computation.2 | async-start | bytes 131072 | tf_op jit(solution)/shard_map/all_to_all | solution.py:44
  1170.9 13.8 %all-to-all-start = ((f32[32,1,512]{2,1,0:T(1,128)}), f32[32,1,512]{2,1,0:T(1,128)S(1)}, u32[]{:S(2)}, u32[]{:S(2)}) async-start(f32[32,1,512]{2,1,0:T(1,128)} %reshape.26), calls=%async_computation | async-start | bytes 131072 | tf_op jit(solution)/shard_map/all_to_all | solution.py:43
  (8 other events, 243.5 us)
Sparse Core Ops, SparseCore 0:
  1071.7 72.2 all-reduce.1
where the time goes:
time: 1200 us; the launch traced here: 1190 us
  blocking collectives  984 us (82%)
  matrix products  56.4 us (5%)
  waiting for transfers between devices  44.8 us (4%)
  local copies, waits for them, and re-layouts  44.5 us (4%)
  starting transfers between devices  29.1 us (2%)
  loops' own time  17.9 us (1%)
  between operations  13.7 us (1%)
    all_gather x24, blocking collectives, whole_step(): whole_rows = lax.all_gather(row_block, 'pairs', axis=1, tiled=True)  957 us
    dot_general x24, matrix products, both_sides(): jnp.einsum('pac,picb->iab', row_block, mixed_terms, precision=highest)  30.3 us
    psum x1, blocking collectives, shards(): particle, coupling = lax.psum((particle, coupling), 'aux')  26.1 us
    dot_general x24, matrix products, both_sides(): jnp.einsum('icd,pbd->picb', amps, row_block, precision=highest)  24.8 us
  transfers between devices with their start and end apart: 5, of which 4 were waited for; matrix products, arithmetic and copies ran while one was open for 1% of the time, Pallas kernels for 0%

commit v1 on v0

--- a/solution.py
+++ b/solution.py
@@ -25,7 +25,9 @@
 
     def whole_step(running, block_index):
         row_block = lax.dynamic_slice_in_dim(factors, block_index * 2, 2, 0)
-        whole_rows = lax.all_gather(row_block, "pairs", axis=1, tiled=True)
+        whole_rows = jnp.concatenate(
+            lax.all_to_all(jnp.stack([row_block] * lax.axis_size("pairs")), "pairs", 0, 0), axis=1
+        )
         return (both_sides(running, amplitudes, whole_rows), None)
 
     particle, unused = lax.scan(

time: 1200 us -> 812 us (0.68)
  blocking collectives: 984 us -> 27 us
  waiting for transfers between devices: 44.8 us -> 452 us
  starting transfers between devices: 29.1 us -> 175 us
  local copies, waits for them, and re-layouts: 44.5 us -> 62.7 us
    all_gather x24 -> x0, blocking collectives: 957 us -> none  [whole_step(): whole_rows = lax.all_gather(row_block, 'pairs', axis=1, tiled=True)]
    all_to_all x0 -> x24, waiting for transfers between devices: none -> 408 us  [whole_step(): lax.all_to_all(jnp.stack([row_block] * lax.axis_size('pairs')), 'pairs',...]
    all_to_all x0 -> x24, starting transfers between devices: none -> 147 us  [whole_step(): lax.all_to_all(jnp.stack([row_block] * lax.axis_size('pairs')), 'pairs',...]
    another operation x0 -> x24, local copies, waits for them, and re-layouts: none -> 20.3 us  [whole_step(): jnp.stack([row_block] * lax.axis_size('pairs'))]
  transfers between devices with their start and end apart: 5 -> 29, of which waited for: 4 -> 28; matrix products, arithmetic and copies ran while one was open for 1% -> 1% of each run, Pallas kernels for 0% -> 0%
where the time goes in v1:
time: 812 us; the launch traced here: 805 us
  waiting for transfers between devices  452 us (56%)
  starting transfers between devices  175 us (22%)
  local copies, waits for them, and re-layouts  62.7 us (8%)
  matrix products  56.4 us (7%)
  blocking collectives  27 us (3%)
  loops' own time  14.8 us (2%)
  between operations  13.7 us (2%)
    all_to_all x24, waiting for transfers between devices, whole_step(): lax.all_to_all(jnp.stack([row_block] * lax.axis_size('pairs')), 'pairs',...  408 us
    all_to_all x24, starting transfers between devices, whole_step(): lax.all_to_all(jnp.stack([row_block] * lax.axis_size('pairs')), 'pairs',...  147 us
    dot_general x24, matrix products, both_sides(): jnp.einsum('pac,picb->iab', row_block, mixed_terms, precision=highest)  30.4 us
    psum x1, blocking collectives, shards(): particle, coupling = lax.psum((particle, coupling), 'aux')  27 us
    dot_general x24, matrix products, both_sides(): jnp.einsum('icd,pbd->picb', amps, row_block, precision=highest)  24.8 us
    psum x1, waiting for transfers between devices, shards(): particle, coupling = lax.psum((particle, coupling), 'aux')  21.6 us
    another operation x24, local copies, waits for them, and re-layouts, whole_step(): jnp.stack([row_block] * lax.axis_size('pairs'))  20.3 us
    dynamic_slice x24, local copies, waits for them, and re-layouts, whole_step(): row_block = lax.dynamic_slice_in_dim(factors, block_index * 2, 2, 0)  17.4 us
  transfers between devices with their start and end apart: 29, of which 28 were waited for; matrix products, arithmetic and copies ran while one was open for 1% of the time, Pallas kernels for 0%

profile of v1, /device:TPU:1, one launch (start us, length us, event | category | flops | bytes accessed | tf_op | source)
XLA Modules:
  0.0 805.5 jit_solution(493108633432498514)
XLA Ops:
  6.5 676.2 %while.11 = (s32[]{:T(128)}, f32[2,256,256]{1,2,0:T(8,128)S(1)}, s32[24]{0:T(128)S(1)}, f32[48,8,256]{2,1,0:T(8,128)}, f32[2,256,256]{2,1,0:T(8,128)}, /*index=5*/s32[]{:T(128)}, s32[1]{0:T(128)}, s32[]{:T(128)}, s32[]{:T(128)}) while((s32[]{:T(128)}, f32[2,256,256]{1,2,0:T(8,128)S(1)}, s32[24]{0:T(128)S(1)}, ...), condition=%wide.region_1.2_spmd.clone, body=%wide.region_0.1_spmd.clone.sunk | while | flops 1610874880 | bytes 8962273 | solution.py:33
  22.2 17.0 %all-to-all-done = f32[32,2,8,256]{3,2,1,0:T(8,128)S(1)} async-done(((f32[32,2,8,256]{3,2,1,0:T(8,128)}), f32[32,2,8,256]{3,2,1,0:T(8,128)S(1)}, u32[]{:S(2)}, u32[]{:S(2)}) %all-to-all-start) | async-done | bytes 524320 | tf_op jit(solution)/shard_map/while/body/eval_jaxpr/all_to_all | solution.py:29
  50.0 17.0 %all-to-all-done = f32[32,2,8,256]{3,2,1,0:T(8,128)S(1)} async-done(((f32[32,2,8,256]{3,2,1,0:T(8,128)}), f32[32,2,8,256]{3,2,1,0:T(8,128)S(1)}, u32[]{:S(2)}, u32[]{:S(2)}) %all-to-all-start) | async-done | bytes 524320 | tf_op jit(solution)/shard_map/while/body/eval_jaxpr/all_to_all | solution.py:29
  77.9 17.0 %all-to-all-done = f32[32,2,8,256]{3,2,1,0:T(8,128)S(1)} async-done(((f32[32,2,8,256]{3,2,1,0:T(8,128)}), f32[32,2,8,256]{3,2,1,0:T(8,128)S(1)}, u32[]{:S(2)}, u32[]{:S(2)}) %all-to-all-start) | async-done | bytes 524320 | tf_op jit(solution)/shard_map/while/body/eval_jaxpr/all_to_all | solution.py:29
  105.8 17.0 %all-to-all-done = f32[32,2,8,256]{3,2,1,0:T(8,128)S(1)} async-done(((f32[32,2,8,256]{3,2,1,0:T(8,128)}), f32[32,2,8,256]{3,2,1,0:T(8,128)S(1)}, u32[]{:S(2)}, u32[]{:S(2)}) %all-to-all-start) | async-done | bytes 524320 | tf_op jit(solution)/shard_map/while/body/eval_jaxpr/all_to_all | solution.py:29
  133.7 17.0 %all-to-all-done = f32[32,2,8,256]{3,2,1,0:T(8,128)S(1)} async-done(((f32[32,2,8,256]{3,2,1,0:T(8,128)}), f32[32,2,8,256]{3,2,1,0:T(8,128)S(1)}, u32[]{:S(2)}, u32[]{:S(2)}) %all-to-all-start) | async-done | bytes 524320 | tf_op jit(solution)/shard_map/while/body/eval_jaxpr/all_to_all | solution.py:29
  161.6 17.0 %all-to-all-done = f32[32,2,8,256]{3,2,1,0:T(8,128)S(1)} async-done(((f32[32,2,8,256]{3,2,1,0:T(8,128)}), f32[32,2,8,256]{3,2,1,0:T(8,128)S(1)}, u32[]{:S(2)}, u32[]{:S(2)}) %all-to-all-start) | async-done | bytes 524320 | tf_op jit(solution)/shard_map/while/body/eval_jaxpr/all_to_all | solution.py:29
  189.5 17.0 %all-to-all-done = f32[32,2,8,256]{3,2,1,0:T(8,128)S(1)} async-done(((f32[32,2,8,256]{3,2,1,0:T(8,128)}), f32[32,2,8,256]{3,2,1,0:T(8,128)S(1)}, u32[]{:S(2)}, u32[]{:S(2)}) %all-to-all-start) | async-done | bytes 524320 | tf_op jit(solution)/shard_map/while/body/eval_jaxpr/all_to_all | solution.py:29
  217.3 17.0 %all-to-all-done = f32[32,2,8,256]{3,2,1,0:T(8,128)S(1)} async-done(((f32[32,2,8,256]{3,2,1,0:T(8,128)}), f32[32,2,8,256]{3,2,1,0:T(8,128)S(1)}, u32[]{:S(2)}, u32[]{:S(2)}) %all-to-all-start) | async-done | bytes 524320 | tf_op jit(solution)/shard_map/while/body/eval_jaxpr/all_to_all | solution.py:29
  245.2 17.0 %all-to-all-done = f32[32,2,8,256]{3,2,1,0:T(8,128)S(1)} async-done(((f32[32,2,8,256]{3,2,1,0:T(8,128)}), f32[32,2,8,256]{3,2,1,0:T(8,128)S(1)}, u32[]{:S(2)}, u32[]{:S(2)}) %all-to-all-start) | async-done | bytes 524320 | tf_op jit(solution)/shard_map/while/body/eval_jaxpr/all_to_all | solution.py:29
  273.1 17.0 %all-to-all-done = f32[32,2,8,256]{3,2,1,0:T(8,128)S(1)} async-done(((f32[32,2,8,256]{3,2,1,0:T(8,128)}), f32[32,2,8,256]{3,2,1,0:T(8,128)S(1)}, u32[]{:S(2)}, u32[]{:S(2)}) %all-to-all-start) | async-done | bytes 524320 | tf_op jit(solution)/shard_map/while/body/eval_jaxpr/all_to_all | solution.py:29
  301.0 17.0 %all-to-all-done = f32[32,2,8,256]{3,2,1,0:T(8,128)S(1)} async-done(((f32[32,2,8,256]{3,2,1,0:T(8,128)}), f32[32,2,8,256]{3,2,1,0:T(8,128)S(1)}, u32[]{:S(2)}, u32[]{:S(2)}) %all-to-all-start) | async-done | bytes 524320 | tf_op jit(solution)/shard_map/while/body/eval_jaxpr/all_to_all | solution.py:29
  328.9 17.0 %all-to-all-done = f32[32,2,8,256]{3,2,1,0:T(8,128)S(1)} async-done(((f32[32,2,8,256]{3,2,1,0:T(8,128)}), f32[32,2,8,256]{3,2,1,0:T(8,128)S(1)}, u32[]{:S(2)}, u32[]{:S(2)}) %all-to-all-start) | async-done | bytes 524320 | tf_op jit(solution)/shard_map/while/body/eval_jaxpr/all_to_all | solution.py:29
  356.7 17.0 %all-to-all-done = f32[32,2,8,256]{3,2,1,0:T(8,128)S(1)} async-done(((f32[32,2,8,256]{3,2,1,0:T(8,128)}), f32[32,2,8,256]{3,2,1,0:T(8,128)S(1)}, u32[]{:S(2)}, u32[]{:S(2)}) %all-to-all-start) | async-done | bytes 524320 | tf_op jit(solution)/shard_map/while/body/eval_jaxpr/all_to_all | solution.py:29
  384.6 17.0 %all-to-all-done = f32[32,2,8,256]{3,2,1,0:T(8,128)S(1)} async-done(((f32[32,2,8,256]{3,2,1,0:T(8,128)}), f32[32,2,8,256]{3,2,1,0:T(8,128)S(1)}, u32[]{:S(2)}, u32[]{:S(2)}) %all-to-all-start) | async-done | bytes 524320 | tf_op jit(solution)/shard_map/while/body/eval_jaxpr/all_to_all | solution.py:29
  412.5 17.0 %all-to-all-done = f32[32,2,8,256]{3,2,1,0:T(8,128)S(1)} async-done(((f32[32,2,8,256]{3,2,1,0:T(8,128)}), f32[32,2,8,256]{3,2,1,0:T(8,128)S(1)}, u32[]{:S(2)}, u32[]{:S(2)}) %all-to-all-start) | async-done | bytes 524320 | tf_op jit(solution)/shard_map/while/body/eval_jaxpr/all_to_all | solution.py:29
  440.4 17.0 %all-to-all-done = f32[32,2,8,256]{3,2,1,0:T(8,128)S(1)} async-done(((f32[32,2,8,256]{3,2,1,0:T(8,128)}), f32[32,2,8,256]{3,2,1,0:T(8,128)S(1)}, u32[]{:S(2)}, u32[]{:S(2)}) %all-to-all-start) | async-done | bytes 524320 | tf_op jit(solution)/shard_map/while/body/eval_jaxpr/all_to_all | solution.py:29
  468.3 17.0 %all-to-all-done = f32[32,2,8,256]{3,2,1,0:T(8,128)S(1)} async-done(((f32[32,2,8,256]{3,2,1,0:T(8,128)}), f32[32,2,8,256]{3,2,1,0:T(8,128)S(1)}, u32[]{:S(2)}, u32[]{:S(2)}) %all-to-all-start) | async-done | bytes 524320 | tf_op jit(solution)/shard_map/while/body/eval_jaxpr/all_to_all | solution.py:29
  496.2 17.0 %all-to-all-done = f32[32,2,8,256]{3,2,1,0:T(8,128)S(1)} async-done(((f32[32,2,8,256]{3,2,1,0:T(8,128)}), f32[32,2,8,256]{3,2,1,0:T(8,128)S(1)}, u32[]{:S(2)}, u32[]{:S(2)}) %all-to-all-start) | async-done | bytes 524320 | tf_op jit(solution)/shard_map/while/body/eval_jaxpr/all_to_all | solution.py:29
  524.0 17.0 %all-to-all-done = f32[32,2,8,256]{3,2,1,0:T(8,128)S(1)} async-done(((f32[32,2,8,256]{3,2,1,0:T(8,128)}), f32[32,2,8,256]{3,2,1,0:T(8,128)S(1)}, u32[]{:S(2)}, u32[]{:S(2)}) %all-to-all-start) | async-done | bytes 524320 | tf_op jit(solution)/shard_map/while/body/eval_jaxpr/all_to_all | solution.py:29
  607.7 17.0 %all-to-all-done = f32[32,2,8,256]{3,2,1,0:T(8,128)S(1)} async-done(((f32[32,2,8,256]{3,2,1,0:T(8,128)}), f32[32,2,8,256]{3,2,1,0:T(8,128)S(1)}, u32[]{:S(2)}, u32[]{:S(2)}) %all-to-all-start) | async-done | bytes 524320 | tf_op jit(solution)/shard_map/while/body/eval_jaxpr/all_to_all | solution.py:29
  635.6 17.0 %all-to-all-done = f32[32,2,8,256]{3,2,1,0:T(8,128)S(1)} async-done(((f32[32,2,8,256]{3,2,1,0:T(8,128)}), f32[32,2,8,256]{3,2,1,0:T(8,128)S(1)}, u32[]{:S(2)}, u32[]{:S(2)}) %all-to-all-start) | async-done | bytes 524320 | tf_op jit(solution)/shard_map/while/body/eval_jaxpr/all_to_all | solution.py:29
  705.4 27.0 %psum.15 = f32[64,64]{1,0:T(8,128)S(1)} all-reduce(f32[64,64]{1,0:T(8,128)S(1)} %reshape.19), channel_id=1, replica_groups=mesh['pairs'=32,'aux'=8] {'aux'}, use_global_device_ids=true, to_apply=%region_3.4 | all-reduce | flops 4096 | bytes 32768 | tf_op jit(solution)/shard_map/psum | solution.py:41
  734.2 21.6 %all-reduce.2.cloned.1.call-done = f32[2,256,256]{2,0,1:T(2,128)} async-done(((f32[2,256,256]{2,0,1:T(2,128)}), f32[2,256,256]{2,0,1:T(2,128)}) %all-reduce.2.cloned.1.call-update) | async-done | bytes 524304 | tf_op jit(solution)/shard_map/psum | solution.py:41
  (256 shorter events, 371.3 us)
Async XLA Ops:
  6.5 749.3 %all-reduce.2.cloned.1.call-start = ((), (), s32[]{:S(2)}) async-start(), calls=%async_computation.5 | async-start | bytes 1048576 | tf_op jit(solution)/shard_map/psum | solution.py:41
  9.3 29.9 %all-to-all-start = ((f32[32,2,8,256]{3,2,1,0:T(8,128)}), f32[32,2,8,256]{3,2,1,0:T(8,128)S(1)}, u32[]{:S(2)}, u32[]{:S(2)}) async-start(f32[32,2,8,256]{3,2,1,0:T(8,128)} %stack.4), calls=%async_computation | async-start | bytes 1048576 | tf_op jit(solution)/shard_map/while/body/eval_jaxpr/all_to_all | solution.py:29
  44.2 22.8 %all-to-all-start = ((f32[32,2,8,256]{3,2,1,0:T(8,128)}), f32[32,2,8,256]{3,2,1,0:T(8,128)S(1)}, u32[]{:S(2)}, u32[]{:S(2)}) async-start(f32[32,2,8,256]{3,2,1,0:T(8,128)} %stack.4), calls=%async_computation | async-start | bytes 1048576 | tf_op jit(solution)/shard_map/while/body/eval_jaxpr/all_to_all | solution.py:29
  72.1 22.8 %all-to-all-start = ((f32[32,2,8,256]{3,2,1,0:T(8,128)}), f32[32,2,8,256]{3,2,1,0:T(8,128)S(1)}, u32[]{:S(2)}, u32[]{:S(2)}) async-start(f32[32,2,8,256]{3,2,1,0:T(8,128)} %stack.4), calls=%async_computation | async-start | bytes 1048576 | tf_op jit(solution)/shard_map/while/body/eval_jaxpr/all_to_all | solution.py:29
  100.0 22.8 %all-to-all-start = ((f32[32,2,8,256]{3,2,1,0:T(8,128)}), f32[32,2,8,256]{3,2,1,0:T(8,128)S(1)}, u32[]{:S(2)}, u32[]{:S(2)}) async-start(f32[32,2,8,256]{3,2,1,0:T(8,128)} %stack.4), calls=%async_computation | async-start | bytes 1048576 | tf_op jit(solution)/shard_map/while/body/eval_jaxpr/all_to_all | solution.py:29
  127.9 22.8 %all-to-all-start = ((f32[32,2,8,256]{3,2,1,0:T(8,128)}), f32[32,2,8,256]{3,2,1,0:T(8,128)S(1)}, u32[]{:S(2)}, u32[]{:S(2)}) async-start(f32[32,2,8,256]{3,2,1,0:T(8,128)} %stack.4), calls=%async_computation | async-start | bytes 1048576 | tf_op jit(solution)/shard_map/while/body/eval_jaxpr/all_to_all | solution.py:29
  155.7 22.8 %all-to-all-start = ((f32[32,2,8,256]{3,2,1,0:T(8,128)}), f32[32,2,8,256]{3,2,1,0:T(8,128)S(1)}, u32[]{:S(2)}, u32[]{:S(2)}) async-start(f32[32,2,8,256]{3,2,1,0:T(8,128)} %stack.4), calls=%async_computation | async-start | bytes 1048576 | tf_op jit(solution)/shard_map/while/body/eval_jaxpr/all_to_all | solution.py:29
  183.6 22.8 %all-to-all-start = ((f32[32,2,8,256]{3,2,1,0:T(8,128)}), f32[32,2,8,256]{3,2,1,0:T(8,128)S(1)}, u32[]{:S(2)}, u32[]{:S(2)}) async-start(f32[32,2,8,256]{3,2,1,0:T(8,128)} %stack.4), calls=%async_computation | async-start | bytes 1048576 | tf_op jit(solution)/shard_map/while/body/eval_jaxpr/all_to_all | solution.py:29
  211.5 22.8 %all-to-all-start = ((f32[32,2,8,256]{3,2,1,0:T(8,128)}), f32[32,2,8,256]{3,2,1,0:T(8,128)S(1)}, u32[]{:S(2)}, u32[]{:S(2)}) async-start(f32[32,2,8,256]{3,2,1,0:T(8,128)} %stack.4), calls=%async_computation | async-start | bytes 1048576 | tf_op jit(solution)/shard_map/while/body/eval_jaxpr/all_to_all | solution.py:29
  239.4 22.8 %all-to-all-start = ((f32[32,2,8,256]{3,2,1,0:T(8,128)}), f32[32,2,8,256]{3,2,1,0:T(8,128)S(1)}, u32[]{:S(2)}, u32[]{:S(2)}) async-start(f32[32,2,8,256]{3,2,1,0:T(8,128)} %stack.4), calls=%async_computation | async-start | bytes 1048576 | tf_op jit(solution)/shard_map/while/body/eval_jaxpr/all_to_all | solution.py:29
  267.3 22.8 %all-to-all-start = ((f32[32,2,8,256]{3,2,1,0:T(8,128)}), f32[32,2,8,256]{3,2,1,0:T(8,128)S(1)}, u32[]{:S(2)}, u32[]{:S(2)}) async-start(f32[32,2,8,256]{3,2,1,0:T(8,128)} %stack.4), calls=%async_computation | async-start | bytes 1048576 | tf_op jit(solution)/shard_map/while/body/eval_jaxpr/all_to_all | solution.py:29
  295.2 22.8 %all-to-all-start = ((f32[32,2,8,256]{3,2,1,0:T(8,128)}), f32[32,2,8,256]{3,2,1,0:T(8,128)S(1)}, u32[]{:S(2)}, u32[]{:S(2)}) async-start(f32[32,2,8,256]{3,2,1,0:T(8,128)} %stack.4), calls=%async_computation | async-start | bytes 1048576 | tf_op jit(solution)/shard_map/while/body/eval_jaxpr/all_to_all | solution.py:29
  323.0 22.8 %all-to-all-start = ((f32[32,2,8,256]{3,2,1,0:T(8,128)}), f32[32,2,8,256]{3,2,1,0:T(8,128)S(1)}, u32[]{:S(2)}, u32[]{:S(2)}) async-start(f32[32,2,8,256]{3,2,1,0:T(8,128)} %stack.4), calls=%async_computation | async-start | bytes 1048576 | tf_op jit(solution)/shard_map/while/body/eval_jaxpr/all_to_all | solution.py:29
  350.9 22.8 %all-to-all-start = ((f32[32,2,8,256]{3,2,1,0:T(8,128)}), f32[32,2,8,256]{3,2,1,0:T(8,128)S(1)}, u32[]{:S(2)}, u32[]{:S(2)}) async-start(f32[32,2,8,256]{3,2,1,0:T(8,128)} %stack.4), calls=%async_computation | async-start | bytes 1048576 | tf_op jit(solution)/shard_map/while/body/eval_jaxpr/all_to_all | solution.py:29
  378.8 22.8 %all-to-all-start = ((f32[32,2,8,256]{3,2,1,0:T(8,128)}), f32[32,2,8,256]{3,2,1,0:T(8,128)S(1)}, u32[]{:S(2)}, u32[]{:S(2)}) async-start(f32[32,2,8,256]{3,2,1,0:T(8,128)} %stack.4), calls=%async_computation | async-start | bytes 1048576 | tf_op jit(solution)/shard_map/while/body/eval_jaxpr/all_to_all | solution.py:29
  406.7 22.8 %all-to-all-start = ((f32[32,2,8,256]{3,2,1,0:T(8,128)}), f32[32,2,8,256]{3,2,1,0:T(8,128)S(1)}, u32[]{:S(2)}, u32[]{:S(2)}) async-start(f32[32,2,8,256]{3,2,1,0:T(8,128)} %stack.4), calls=%async_computation | async-start | bytes 1048576 | tf_op jit(solution)/shard_map/while/body/eval_jaxpr/all_to_all | solution.py:29
  434.6 22.8 %all-to-all-start = ((f32[32,2,8,256]{3,2,1,0:T(8,128)}), f32[32,2,8,256]{3,2,1,0:T(8,128)S(1)}, u32[]{:S(2)}, u32[]{:S(2)}) async-start(f32[32,2,8,256]{3,2,1,0:T(8,128)} %stack.4), calls=%async_computation | async-start | bytes 1048576 | tf_op jit(solution)/shard_map/while/body/eval_jaxpr/all_to_all | solution.py:29
  490.3 22.8 %all-to-all-start = ((f32[32,2,8,256]{3,2,1,0:T(8,128)}), f32[32,2,8,256]{3,2,1,0:T(8,128)S(1)}, u32[]{:S(2)}, u32[]{:S(2)}) async-start(f32[32,2,8,256]{3,2,1,0:T(8,128)} %stack.4), calls=%async_computation | async-start | bytes 1048576 | tf_op jit(solution)/shard_map/while/body/eval_jaxpr/all_to_all | solution.py:29
  518.2 22.8 %all-to-all-start = ((f32[32,2,8,256]{3,2,1,0:T(8,128)}), f32[32,2,8,256]{3,2,1,0:T(8,128)S(1)}, u32[]{:S(2)}, u32[]{:S(2)}) async-start(f32[32,2,8,256]{3,2,1,0:T(8,128)} %stack.4), calls=%async_computation | async-start | bytes 1048576 | tf_op jit(solution)/shard_map/while/body/eval_jaxpr/all_to_all | solution.py:29
  546.1 22.8 %all-to-all-start = ((f32[32,2,8,256]{3,2,1,0:T(8,128)}), f32[32,2,8,256]{3,2,1,0:T(8,128)S(1)}, u32[]{:S(2)}, u32[]{:S(2)}) async-start(f32[32,2,8,256]{3,2,1,0:T(8,128)} %stack.4), calls=%async_computation | async-start | bytes 1048576 | tf_op jit(solution)/shard_map/while/body/eval_jaxpr/all_to_all | solution.py:29
  601.9 22.8 %all-to-all-start = ((f32[32,2,8,256]{3,2,1,0:T(8,128)}), f32[32,2,8,256]{3,2,1,0:T(8,128)S(1)}, u32[]{:S(2)}, u32[]{:S(2)}) async-start(f32[32,2,8,256]{3,2,1,0:T(8,128)} %stack.4), calls=%async_computation | async-start | bytes 1048576 | tf_op jit(solution)/shard_map/while/body/eval_jaxpr/all_to_all | solution.py:29
  629.7 22.8 %all-to-all-start = ((f32[32,2,8,256]{3,2,1,0:T(8,128)}), f32[32,2,8,256]{3,2,1,0:T(8,128)S(1)}, u32[]{:S(2)}, u32[]{:S(2)}) async-start(f32[32,2,8,256]{3,2,1,0:T(8,128)} %stack.4), calls=%async_computation | async-start | bytes 1048576 | tf_op jit(solution)/shard_map/while/body/eval_jaxpr/all_to_all | solution.py:29
  701.5 56.3 %all-to-all-start.2 = ((f32[32,1,512]{2,1,0:T(1,128)}), f32[32,1,512]{2,1,0:T(1,128)S(1)}, u32[]{:S(2)}, u32[]{:S(2)}) async-start(f32[32,1,512]{2,1,0:T(1,128)} %reshape.38), calls=%async_computation.2 | async-start | bytes 131072 | tf_op jit(solution)/shard_map/all_to_all | solution.py:47
  757.8 25.0 %all-to-all-start.3 = ((f32[32,1,512]{2,1,0:T(1,128)}), f32[32,1,512]{2,1,0:T(1,128)S(1)}, u32[]{:S(2)}, u32[]{:S(2)}) async-start(f32[32,1,512]{2,1,0:T(1,128)} %reshape.32), calls=%async_computation.3 | async-start | bytes 131072 | tf_op jit(solution)/shard_map/all_to_all | solution.py:46
  (32 other events, 1340.1 us)
Sparse Core Ops, SparseCore 0:
  683.9 71.8 all-reduce.1
